TPU v7x, 512 devices: a whole 4x4x16 slice. The times are simulated.
512 devices in a mesh: dp: 2 (over x_lo), seq: 32 (over z, core), tensor: 8 (over y, x_hi).
Axes of the slice: x: 4 (x_hi: 2, x_lo: 2; x = x_hi * 2 + x_lo), y: 4, z: 16, core: 2. Of those that a mesh axis runs over, the one named last changes fastest.
Arguments:
- queries: bfloat16 [2, 4096, 3072], P('dp', 'seq', 'tensor'), may hold values from -24 to 24
- keys: bfloat16 [2, 8192, 3072], P('dp', 'seq', 'tensor'), may hold values from -8 to 8
- values: bfloat16 [2, 8192, 3072], P('dp', 'seq', 'tensor'), may hold values from -160 to 160
- grad_out: bfloat16 [2, 4096, 3072], P('dp', 'seq', 'tensor'), may hold values from -60 to 60
- gain: float32 [3072], P('tensor'), may hold values from 0.1 to 1.9
- band_start: int32 [2, 32], P('dp', 'seq'), may hold values from 0 to 62, as said below
- band_end: int32 [2, 32], P('dp', 'seq'), may hold values from 6 to 64
Outputs:
- attended: bfloat16 [2, 4096, 3072], P('dp', 'seq', 'tensor')
- grad_queries: bfloat16 [2, 4096, 3072], P('dp', 'seq', 'tensor')
- grad_keys: bfloat16 [2, 8192, 3072], P('dp', 'seq', 'tensor')
- grad_values: bfloat16 [2, 8192, 3072], P('dp', 'seq', 'tensor')
- grad_gain: float32 [3072], P('tensor')
Inputs may be any that keep to these rules, and one draw needn't show every extreme that they name: Along the token blocks of a recording band_start and band_end never fall and band_start < band_end; the band of a token block held by seq index j lies within encoder blocks (j - 2) * (2) to (j + 3) * 2 - 1, and in every draw some bands reach both of these limits.
All inputs are finite; a program needn't handle non-finite values.
Results may differ from a plain program's by a relative error of at most 0.008.
Values may be sent and summed in bfloat16 or wider, within the bound.
No kernel may reach another device: no remote copies, remote signals or barrier semaphores. Data moves between devices by JAX's collectives and lax.ppermute only.
A program may use at most 64 MiB of HBM per device.

v0:
```python
import jax
import jax.numpy as jnp
from jax import lax
from jax.sharding import PartitionSpec as P

D = 3072
HD = 96
TB = 128
EB = 128
REACH = 2
epsilon = 1e-06


def shifted(array, axis, by):
    size = lax.axis_size(axis)
    pairs = [(i, i + by) for i in range(size) if 0 <= i + by < size]
    return lax.ppermute(array, axis, pairs)


def head_probs(query_head, key_head, allowed, scale):
    scores = (
        lax.dot_general(
            query_head, key_head, (((1,), (1,)), ((), ())), preferred_element_type=jnp.float32
        )
        * scale
    )
    scores = jnp.where(allowed, scores, -jnp.inf)
    top = jnp.max(scores, axis=1, keepdims=True)
    weights = jnp.exp(scores - top)
    return weights / jnp.sum(weights, axis=1, keepdims=True)


def per_device(queries, keys, values, grad_out, gain, band_start, band_end):
    query_local = queries[0]
    key_local = keys[0]
    value_local = values[0]
    grad_local = grad_out[0].astype(jnp.float32)
    starts = band_start[0]
    ends = band_end[0]
    tok_rows, width = query_local.shape
    frame_rows = key_local.shape[0]
    heads = width // HD
    scale = HD ** (-0.5)
    here = lax.axis_index("seq")
    pair = jnp.stack([key_local, value_local])
    pieces = []
    for offset in range(-REACH, REACH + 1):
        if offset == 0:
            pieces.append(pair)
        else:
            pieces.append(shifted(pair, "seq", -offset))
    window = jnp.concatenate(pieces, axis=1)
    key_window = window[0]
    value_window = window[1]
    span = key_window.shape[0]
    frame_block = ((here - REACH) * frame_rows + jnp.arange(span, dtype=jnp.int32)) // EB
    row_start = jnp.repeat(starts, TB)
    row_end = jnp.repeat(ends, TB)
    allowed = (frame_block[None, :] >= row_start[:, None]) & (
        frame_block[None, :] < row_end[:, None]
    )
    outputs = []
    kept_probs = []
    for head in range(heads):
        columns = slice(head * HD, (head + 1) * HD)
        probs = head_probs(query_local[:, columns], key_window[:, columns], allowed, scale)
        kept_probs.append(probs)
        outputs.append(
            jnp.dot(
                probs.astype(jnp.bfloat16),
                value_window[:, columns],
                preferred_element_type=jnp.float32,
            )
        )
    attn = jnp.concatenate(outputs, axis=1)
    scaled_grad = grad_local * gain[None, :]
    square_local = jnp.sum(attn * attn, axis=1)
    cross_local = jnp.sum(scaled_grad * attn, axis=1)
    square_total = lax.psum(square_local, "tensor")
    inv_rms = lax.rsqrt(square_total / D + epsilon)
    normed = attn * inv_rms[:, None]
    attended = (normed * gain[None, :]).astype(jnp.bfloat16)
    cross_total = lax.psum(cross_local, "tensor")
    mean_cross = inv_rms * cross_total / D
    grad_attn = (inv_rms[:, None] * (scaled_grad - normed * mean_cross[:, None])).astype(
        jnp.bfloat16
    )
    grad_gain = lax.psum(jnp.sum(grad_local * normed, axis=0), ("dp", "seq"))
    query_grads = []
    key_grads = []
    value_grads = []
    for head in range(heads):
        columns = slice(head * HD, (head + 1) * HD)
        query_head = query_local[:, columns]
        key_head = key_window[:, columns]
        value_head = value_window[:, columns]
        grad_head = grad_attn[:, columns]
        probs = kept_probs[head]
        probs_b = probs.astype(jnp.bfloat16)
        grad_probs = lax.dot_general(
            grad_head, value_head, (((1,), (1,)), ((), ())), preferred_element_type=jnp.float32
        )
        inner = jnp.sum(probs * grad_probs, axis=1, keepdims=True)
        grad_scores = (probs * (grad_probs - inner)).astype(jnp.bfloat16)
        query_grads.append(
            scale * jnp.dot(grad_scores, key_head, preferred_element_type=jnp.float32)
        )
        key_grads.append(
            scale
            * lax.dot_general(
                grad_scores,
                query_head,
                (((0,), (0,)), ((), ())),
                preferred_element_type=jnp.float32,
            )
        )
        value_grads.append(
            lax.dot_general(
                probs_b, grad_head, (((0,), (0,)), ((), ())), preferred_element_type=jnp.float32
            )
        )
    grad_queries = jnp.concatenate(query_grads, axis=1).astype(jnp.bfloat16)
    window_grads = jnp.stack(
        [jnp.concatenate(key_grads, axis=1), jnp.concatenate(value_grads, axis=1)]
    )
    parts = [
        window_grads[:, index * frame_rows : (index + 1) * frame_rows]
        for index in range(2 * REACH + 1)
    ]
    total = parts[REACH]
    for offset in range(-REACH, REACH + 1):
        if offset != 0:
            total = total + shifted(
                parts[REACH + offset].astype(jnp.bfloat16), "seq", offset
            ).astype(jnp.float32)
    grad_keys = total[0].astype(jnp.bfloat16)
    grad_values = total[1].astype(jnp.bfloat16)
    return (attended[None], grad_queries[None], grad_keys[None], grad_values[None], grad_gain)


def solution(mesh):
    return jax.shard_map(
        per_device,
        mesh=mesh,
        in_specs=(
            P("dp", "seq", "tensor"),
            P("dp", "seq", "tensor"),
            P("dp", "seq", "tensor"),
            P("dp", "seq", "tensor"),
            P("tensor"),
            P("dp", "seq"),
            P("dp", "seq"),
        ),
        out_specs=(
            P("dp", "seq", "tensor"),
            P("dp", "seq", "tensor"),
            P("dp", "seq", "tensor"),
            P("dp", "seq", "tensor"),
            P("tensor"),
        ),
        check_vma=False,
    )
```

profile of v0, /device:TPU:6, one launch (start us, length us, event | category | flops | bytes accessed | tf_op | source)
XLA Modules:
  0.0 224.1 jit_solution(527827791470561601)
XLA Ops:
  2.6 3.8 %collective-permute-start = (bf16[2,256,384]{2,1,0:T(8,128)(2,1)S(1)}, bf16[2,256,384]{2,1,0:T(8,128)(2,1)S(1)}, u32[]{:S(2)}, u32[]{:S(2)}) collective-permute-start(bf16[2,256,384]{2,1,0:T(8,128)(2,1)S(1)} %constant_dynamic-update-slice_fusion), channel_id=1, source_target_pairs={{0,16},{8,24},{16,32},{24,40},{32,48},{40,56},{48,64},{56,72},{64,... | collective-permute-start | bytes 1179656 | tf_op jit(solution)/shard_map/ppermute | solution.py:17
  6.5 1.5 collective-permute-start.1
  8.0 1.3 collective-permute-start.2
  9.3 1.3 collective-permute-start.3
  12.9 3.0 %collective-permute-done = bf16[2,256,384]{2,1,0:T(8,128)(2,1)S(1)} collective-permute-done((bf16[2,256,384]{2,1,0:T(8,128)(2,1)S(1)}, bf16[2,256,384]{2,1,0:T(8,128)(2,1)S(1)}, u32[]{:S(2)}, u32[]{:S(2)}) %collective-permute-start) | collective-permute-done | bytes 393248 | tf_op jit(solution)/shard_map/ppermute | solution.py:17
  16.2 11.9 %collective-permute-done.3 = bf16[2,256,384]{2,1,0:T(8,128)(2,1)S(1)} collective-permute-done((bf16[2,256,384]{2,1,0:T(8,128)(2,1)S(1)}, bf16[2,256,384]{2,1,0:T(8,128)(2,1)S(1)}, u32[]{:S(2)}, u32[]{:S(2)}) %collective-permute-start.3) | collective-permute-done | bytes 393248 | tf_op jit(solution)/shard_map/ppermute | solution.py:17
  33.1 20.7 %psum.21 = f32[128]{0:T(128)S(1)} all-reduce(f32[128]{0:T(128)S(1)} %multiply_reduce_fusion), channel_id=1, replica_groups=mesh['dp'=2,'seq'=32,'tensor'=8] {'tensor'}, use_global_device_ids=true, to_apply=%region_9.10 | all-reduce | flops 128 | bytes 1024 | tf_op jit(solution)/shard_map/psum | solution.py:79
  54.1 23.3 %psum.22 = f32[128]{0:T(128)S(1)} all-reduce(f32[128]{0:T(128)S(1)} %get-tuple-element.11), channel_id=1, replica_groups=mesh['dp'=2,'seq'=32,'tensor'=8] {'tensor'}, use_global_device_ids=true, to_apply=%region_11.12 | all-reduce | flops 128 | bytes 1024 | tf_op jit(solution)/shard_map/psum | solution.py:83
  77.5 1.4 fusion.19
  79.3 1.2 fusion.23
  80.5 1.1 fusion.25
  83.1 1.2 convolution_multiply_fusion.5
  84.3 1.1 fusion.70
  85.3 1.1 fusion.69
  86.4 1.0 fusion.68
  87.4 1.1 fusion.67
  89.4 1.2 fusion.24
  94.5 1.0 fusion.98
  95.6 3.8 %collective-permute-start.7 = (bf16[2,256,384]{1,2,0:T(8,128)(2,1)}, bf16[2,256,384]{1,2,0:T(8,128)(2,1)S(1)}, u32[]{:S(2)}, u32[]{:S(2)}) collective-permute-start(bf16[2,256,384]{1,2,0:T(8,128)(2,1)} %get-tuple-element.13), channel_id=1, source_target_pairs={{0,16},{8,24},{16,32},{24,40},{32,48},{40,56},{48,64},{56,72},{64,... | collective-permute-start | bytes 1179656 | tf_op jit(solution)/shard_map/ppermute | solution.py:17
  99.4 2.1 collective-permute-start.6
  101.5 1.3 collective-permute-start.5
  102.8 1.3 collective-permute-start.4
  105.6 115.3 %psum.23 = f32[384]{0:T(512)} all-reduce(f32[384]{0:T(512)S(1)} %get-tuple-element.10), channel_id=1, replica_groups=mesh['dp'=2,'seq'=32,'tensor'=8] {'dp','seq'}, use_global_device_ids=true, to_apply=%region_17.18 | all-reduce | flops 384 | bytes 3072 | tf_op jit(solution)/shard_map/psum | solution.py:88
  220.9 1.6 fusion.18
  (87 shorter events, 18.3 us)
Async XLA Ops:
  0.6 15.4 %copy-start.7 = (bf16[1,256,384]{2,1,0:T(8,128)(2,1)S(1)}, bf16[1,256,384]{2,1,0:T(8,128)(2,1)}, u32[]{:S(2)}) copy-start(bf16[1,256,384]{2,1,0:T(8,128)(2,1)} %param.8) | copy-start | bytes 589828
  0.6 15.5 %copy-start.8 = (bf16[1,256,384]{2,1,0:T(8,128)(2,1)S(1)}, bf16[1,256,384]{2,1,0:T(8,128)(2,1)}, u32[]{:S(2)}) copy-start(bf16[1,256,384]{2,1,0:T(8,128)(2,1)} %param.9) | copy-start | bytes 589828
  2.6 13.3 %collective-permute-start = (bf16[2,256,384]{2,1,0:T(8,128)(2,1)S(1)}, bf16[2,256,384]{2,1,0:T(8,128)(2,1)S(1)}, u32[]{:S(2)}, u32[]{:S(2)}) collective-permute-start(bf16[2,256,384]{2,1,0:T(8,128)(2,1)S(1)} %constant_dynamic-update-slice_fusion), channel_id=1, source_target_pairs={{0,16},{8,24},{16,32},{24,40},{32,48},{40,56},{48,64},{56,72},{64,... | collective-permute-start | bytes 1179656 | tf_op jit(solution)/shard_map/ppermute | solution.py:17
  6.5 9.5 %collective-permute-start.1 = (bf16[2,256,384]{2,1,0:T(8,128)(2,1)S(1)}, bf16[2,256,384]{2,1,0:T(8,128)(2,1)S(1)}, u32[]{:S(2)}, u32[]{:S(2)}) collective-permute-start(bf16[2,256,384]{2,1,0:T(8,128)(2,1)S(1)} %constant_dynamic-update-slice_fusion), channel_id=1, source_target_pairs={{0,8},{8,16},{16,24},{24,32},{32,40},{40,48},{48,56},{56,64},{64,7... | collective-permute-start | bytes 1179656 | tf_op jit(solution)/shard_map/ppermute | solution.py:17
  8.0 8.2 %collective-permute-start.2 = (bf16[2,256,384]{2,1,0:T(8,128)(2,1)S(1)}, bf16[2,256,384]{2,1,0:T(8,128)(2,1)S(1)}, u32[]{:S(2)}, u32[]{:S(2)}) collective-permute-start(bf16[2,256,384]{2,1,0:T(8,128)(2,1)S(1)} %constant_dynamic-update-slice_fusion), channel_id=1, source_target_pairs={{8,0},{16,8},{24,16},{32,24},{40,32},{48,40},{56,48},{64,56},{72,6... | collective-permute-start | bytes 1179656 | tf_op jit(solution)/shard_map/ppermute | solution.py:17
  9.3 18.8 %collective-permute-start.3 = (bf16[2,256,384]{2,1,0:T(8,128)(2,1)S(1)}, bf16[2,256,384]{2,1,0:T(8,128)(2,1)S(1)}, u32[]{:S(2)}, u32[]{:S(2)}) collective-permute-start(bf16[2,256,384]{2,1,0:T(8,128)(2,1)S(1)} %constant_dynamic-update-slice_fusion), channel_id=1, source_target_pairs={{16,0},{24,8},{32,16},{40,24},{48,32},{56,40},{64,48},{72,56},{80,... | collective-permute-start | bytes 1179656 | tf_op jit(solution)/shard_map/ppermute | solution.py:17
  28.2 0.9 copy-start.9
  28.4 2.3 %copy-start.1 = (bf16[1280,384]{1,0:T(8,128)(2,1)}, bf16[1280,384]{1,0:T(8,128)(2,1)S(1)}, u32[]{:S(2)}) copy-start(bf16[1280,384]{1,0:T(8,128)(2,1)S(1)} %get-tuple-element.16) | copy-start | bytes 2949124
  28.4 4.3 %copy-start.5 = (bf16[1280,384]{1,0:T(8,128)(2,1)}, bf16[1280,384]{1,0:T(8,128)(2,1)S(1)}, u32[]{:S(2)}) copy-start(bf16[1280,384]{1,0:T(8,128)(2,1)S(1)} %get-tuple-element.17) | copy-start | bytes 2949124
  32.5 21.3 %copy-start.15 = (f32[384]{0:T(512)S(1)}, f32[384]{0:T(512)}, u32[]{:S(2)}) copy-start(f32[384]{0:T(512)} %param.11) | copy-start | bytes 4612
  77.3 1.6 copy-start.6
  80.5 1.3 copy-start.2
  88.5 2.5 %copy-start.10 = (f32[128,1280]{0,1:T(8,128)S(1)}, f32[128,1280]{0,1:T(8,128)}, u32[]{:S(2)}) copy-start(f32[128,1280]{0,1:T(8,128)} %get-tuple-element.35) | copy-start | bytes 1966084
  90.6 1.0 copy-start.4
  91.6 1.0 copy-start.11
  91.6 1.2 copy-start.12
  91.6 1.3 copy-start.13
  91.6 1.5 copy-start.14
  93.2 1.3 copy-start
  94.5 9.5 %copy-start.3 = (bf16[1280,384]{1,0:T(8,128)(2,1)S(1)}, bf16[1280,384]{1,0:T(8,128)(2,1)}, u32[]{:S(2)}) copy-start(bf16[1280,384]{1,0:T(8,128)(2,1)} %copy-done.1) | copy-start | bytes 2949124
  95.6 125.3 %collective-permute-start.7 = (bf16[2,256,384]{1,2,0:T(8,128)(2,1)}, bf16[2,256,384]{1,2,0:T(8,128)(2,1)S(1)}, u32[]{:S(2)}, u32[]{:S(2)}) collective-permute-start(bf16[2,256,384]{1,2,0:T(8,128)(2,1)} %get-tuple-element.13), channel_id=1, source_target_pairs={{0,16},{8,24},{16,32},{24,40},{32,48},{40,56},{48,64},{56,72},{64,... | collective-permute-start | bytes 1179656 | tf_op jit(solution)/shard_map/ppermute | solution.py:17
  99.4 121.4 %collective-permute-start.6 = (bf16[2,256,384]{1,2,0:T(8,128)(2,1)}, bf16[2,256,384]{1,2,0:T(8,128)(2,1)}, u32[]{:S(2)}, u32[]{:S(2)}) collective-permute-start(bf16[2,256,384]{1,2,0:T(8,128)(2,1)} %get-tuple-element.14), channel_id=1, source_target_pairs={{0,8},{8,16},{16,24},{24,32},{32,40},{40,48},{48,56},{56,64},{64,7... | collective-permute-start | bytes 1179656 | tf_op jit(solution)/shard_map/ppermute | solution.py:17
  101.5 119.4 %collective-permute-start.5 = (bf16[2,256,384]{1,2,0:T(8,128)(2,1)}, bf16[2,256,384]{1,2,0:T(8,128)(2,1)}, u32[]{:S(2)}, u32[]{:S(2)}) collective-permute-start(bf16[2,256,384]{1,2,0:T(8,128)(2,1)} %get-tuple-element.15), channel_id=1, source_target_pairs={{8,0},{16,8},{24,16},{32,24},{40,32},{48,40},{56,48},{64,56},{72,6... | collective-permute-start | bytes 1179656 | tf_op jit(solution)/shard_map/ppermute | solution.py:17
  102.8 118.1 %collective-permute-start.4 = (bf16[2,256,384]{1,2,0:T(8,128)(2,1)S(1)}, bf16[2,256,384]{1,2,0:T(8,128)(2,1)}, u32[]{:S(2)}, u32[]{:S(2)}) collective-permute-start(bf16[2,256,384]{1,2,0:T(8,128)(2,1)S(1)} %get-tuple-element.12), channel_id=1, source_target_pairs={{16,0},{24,8},{32,16},{40,24},{48,32},{56,40},{64,48},{72,56},{80,... | collective-permute-start | bytes 1179656 | tf_op jit(solution)/shard_map/ppermute | solution.py:17
where the time goes:
time: 225 us; the launch traced here: 224 us
  blocking collectives  159 us (71%)
  starting transfers between devices  16.4 us (7%)
  matrix products  15.2 us (7%)
  waiting for transfers between devices  14.9 us (7%)
  local copies, waits for them, and re-layouts  10.8 us (5%)
  other arithmetic  5.26 us (2%)
  between operations  2.34 us (1%)
    psum x1, blocking collectives, per_device(): grad_gain = lax.psum(jnp.sum(grad_local * normed, axis=0), ('dp', 'seq'))  115 us
    psum x1, blocking collectives, per_device(): cross_total = lax.psum(cross_local, 'tensor')  23.3 us
    psum x1, blocking collectives, per_device(): square_total = lax.psum(square_local, 'tensor')  20.7 us
    ppermute x8, starting transfers between devices, shifted(): return lax.ppermute(array, axis, pairs)  16.4 us
    ppermute x8, waiting for transfers between devices, shifted(): return lax.ppermute(array, axis, pairs)  14.9 us
    unnamed x43, local copies, waits for them, and re-layouts  8.52 us
  transfers between devices with their start and end apart: 8, of which 2 were waited for; matrix products, arithmetic and copies ran while one was open for 1% of the time, Pallas kernels for 0%

commit v1 on v0

--- a/solution.py
+++ b/solution.py
@@ -85,7 +85,8 @@
     grad_attn = (inv_rms[:, None] * (scaled_grad - normed * mean_cross[:, None])).astype(
         jnp.bfloat16
     )
-    grad_gain = lax.psum(jnp.sum(grad_local * normed, axis=0), ("dp", "seq"))
+    partial = lax.psum(jnp.sum(grad_local * normed, axis=0), "dp")
+    grad_gain = lax.psum(partial, "seq")
     query_grads = []
     key_grads = []
     value_grads = []

time: 225 us -> 168 us (0.75)
  blocking collectives: 159 us -> 101 us
    psum x1 -> x2, blocking collectives: 115 us -> 57.3 us  [the longest x1 52.4 us: per_device(): grad_gain = lax.psum(partial, 'seq')]
  transfers between devices with their start and end apart: 8 -> 8, of which waited for: 2 -> 2; matrix products, arithmetic and copies ran while one was open for 1% -> 2% of each run, Pallas kernels for 0% -> 0%
where the time goes in v1:
time: 168 us; the launch traced here: 166 us
  blocking collectives  101 us (60%)
  starting transfers between devices  16.4 us (10%)
  matrix products  15.2 us (9%)
  waiting for transfers between devices  14.9 us (9%)
  local copies, waits for them, and re-layouts  10.8 us (6%)
  other arithmetic  5.26 us (3%)
  between operations  2.34 us (1%)
    psum x1, blocking collectives, per_device(): grad_gain = lax.psum(partial, 'seq')  52.4 us
    psum x1, blocking collectives, per_device(): cross_total = lax.psum(cross_local, 'tensor')  23.3 us
    psum x1, blocking collectives, per_device(): square_total = lax.psum(square_local, 'tensor')  20.7 us
    ppermute x8, starting transfers between devices, shifted(): return lax.ppermute(array, axis, pairs)  16.4 us
    ppermute x8, waiting for transfers between devices, shifted(): return lax.ppermute(array, axis, pairs)  14.9 us
    unnamed x43, local copies, waits for them, and re-layouts  8.52 us
    psum x1, blocking collectives, per_device(): partial = lax.psum(jnp.sum(grad_local * normed, axis=0), 'dp')  4.91 us
    dot_general x4, matrix products, per_device(): lax.dot_general(probs_b, grad_head, (((0,), (0,)), ((), ())), preferred_e...  4.21 us
  transfers between devices with their start and end apart: 8, of which 2 were waited for; matrix products, arithmetic and copies ran while one was open for 2% of the time, Pallas kernels for 0%

profile of v1, /device:TPU:6, one launch (start us, length us, event | category | flops | bytes accessed | tf_op | source)
XLA Modules:
  0.0 166.2 jit_solution(12098283196229241054)
XLA Ops:
  2.6 3.8 %collective-permute-start = (bf16[2,256,384]{2,1,0:T(8,128)(2,1)S(1)}, bf16[2,256,384]{2,1,0:T(8,128)(2,1)S(1)}, u32[]{:S(2)}, u32[]{:S(2)}) collective-permute-start(bf16[2,256,384]{2,1,0:T(8,128)(2,1)S(1)} %constant_dynamic-update-slice_fusion), channel_id=1, source_target_pairs={{0,16},{8,24},{16,32},{24,40},{32,48},{40,56},{48,64},{56,72},{64,... | collective-permute-start | bytes 1179656 | tf_op jit(solution)/shard_map/ppermute | solution.py:17
  6.5 1.5 collective-permute-start.1
  8.0 1.3 collective-permute-start.2
  9.3 1.3 collective-permute-start.3
  12.9 3.0 %collective-permute-done = bf16[2,256,384]{2,1,0:T(8,128)(2,1)S(1)} collective-permute-done((bf16[2,256,384]{2,1,0:T(8,128)(2,1)S(1)}, bf16[2,256,384]{2,1,0:T(8,128)(2,1)S(1)}, u32[]{:S(2)}, u32[]{:S(2)}) %collective-permute-start) | collective-permute-done | bytes 393248 | tf_op jit(solution)/shard_map/ppermute | solution.py:17
  16.2 11.9 %collective-permute-done.3 = bf16[2,256,384]{2,1,0:T(8,128)(2,1)S(1)} collective-permute-done((bf16[2,256,384]{2,1,0:T(8,128)(2,1)S(1)}, bf16[2,256,384]{2,1,0:T(8,128)(2,1)S(1)}, u32[]{:S(2)}, u32[]{:S(2)}) %collective-permute-start.3) | collective-permute-done | bytes 393248 | tf_op jit(solution)/shard_map/ppermute | solution.py:17
  33.1 20.7 %psum.28 = f32[128]{0:T(128)S(1)} all-reduce(f32[128]{0:T(128)S(1)} %multiply_reduce_fusion), channel_id=1, replica_groups=mesh['dp'=2,'seq'=32,'tensor'=8] {'tensor'}, use_global_device_ids=true, to_apply=%region_9.10 | all-reduce | flops 128 | bytes 1024 | tf_op jit(solution)/shard_map/psum | solution.py:79
  54.1 23.3 %psum.29 = f32[128]{0:T(128)S(1)} all-reduce(f32[128]{0:T(128)S(1)} %get-tuple-element.11), channel_id=1, replica_groups=mesh['dp'=2,'seq'=32,'tensor'=8] {'tensor'}, use_global_device_ids=true, to_apply=%region_11.12 | all-reduce | flops 128 | bytes 1024 | tf_op jit(solution)/shard_map/psum | solution.py:83
  77.5 1.4 fusion.19
  79.3 1.2 fusion.23
  80.5 1.1 fusion.25
  83.1 1.2 convolution_multiply_fusion.5
  84.3 1.1 fusion.70
  85.3 1.1 fusion.69
  87.4 1.1 fusion.67
  89.4 1.2 fusion.24
  94.5 1.0 fusion.98
  95.6 3.8 %collective-permute-start.7 = (bf16[2,256,384]{1,2,0:T(8,128)(2,1)}, bf16[2,256,384]{1,2,0:T(8,128)(2,1)S(1)}, u32[]{:S(2)}, u32[]{:S(2)}) collective-permute-start(bf16[2,256,384]{1,2,0:T(8,128)(2,1)} %get-tuple-element.13), channel_id=1, source_target_pairs={{0,16},{8,24},{16,32},{24,40},{32,48},{40,56},{48,64},{56,72},{64,... | collective-permute-start | bytes 1179656 | tf_op jit(solution)/shard_map/ppermute | solution.py:17
  99.4 2.1 %collective-permute-start.6 = (bf16[2,256,384]{1,2,0:T(8,128)(2,1)}, bf16[2,256,384]{1,2,0:T(8,128)(2,1)}, u32[]{:S(2)}, u32[]{:S(2)}) collective-permute-start(bf16[2,256,384]{1,2,0:T(8,128)(2,1)} %get-tuple-element.14), channel_id=1, source_target_pairs={{0,8},{8,16},{16,24},{24,32},{32,40},{40,48},{48,56},{56,64},{64,7... | collective-permute-start | bytes 1179656 | tf_op jit(solution)/shard_map/ppermute | solution.py:17
  101.5 1.3 collective-permute-start.5
  102.8 1.3 collective-permute-start.4
  105.6 4.9 %psum.30 = f32[384]{0:T(512)S(1)} all-reduce(f32[384]{0:T(512)S(1)} %get-tuple-element.10), channel_id=1, replica_groups=mesh['dp'=2,'seq'=32,'tensor'=8] {'dp'}, use_global_device_ids=true, to_apply=%region_17.18 | all-reduce | flops 384 | bytes 3072 | tf_op jit(solution)/shard_map/psum | solution.py:88
  110.5 52.4 %psum.31 = f32[384]{0:T(512)} all-reduce(f32[384]{0:T(512)S(1)} %psum.30), channel_id=1, replica_groups=mesh['dp'=2,'seq'=32,'tensor'=8] {'seq'}, use_global_device_ids=true, to_apply=%region_18.19 | all-reduce | flops 384 | bytes 3072 | tf_op jit(solution)/shard_map/psum | solution.py:89
  162.9 1.6 fusion.18
  (88 shorter events, 19.4 us)
Async XLA Ops:
  0.6 15.4 %copy-start.7 = (bf16[1,256,384]{2,1,0:T(8,128)(2,1)S(1)}, bf16[1,256,384]{2,1,0:T(8,128)(2,1)}, u32[]{:S(2)}) copy-start(bf16[1,256,384]{2,1,0:T(8,128)(2,1)} %param.8) | copy-start | bytes 589828
  0.6 15.5 %copy-start.8 = (bf16[1,256,384]{2,1,0:T(8,128)(2,1)S(1)}, bf16[1,256,384]{2,1,0:T(8,128)(2,1)}, u32[]{:S(2)}) copy-start(bf16[1,256,384]{2,1,0:T(8,128)(2,1)} %param.9) | copy-start | bytes 589828
  2.6 13.3 %collective-permute-start = (bf16[2,256,384]{2,1,0:T(8,128)(2,1)S(1)}, bf16[2,256,384]{2,1,0:T(8,128)(2,1)S(1)}, u32[]{:S(2)}, u32[]{:S(2)}) collective-permute-start(bf16[2,256,384]{2,1,0:T(8,128)(2,1)S(1)} %constant_dynamic-update-slice_fusion), channel_id=1, source_target_pairs={{0,16},{8,24},{16,32},{24,40},{32,48},{40,56},{48,64},{56,72},{64,... | collective-permute-start | bytes 1179656 | tf_op jit(solution)/shard_map/ppermute | solution.py:17
  6.5 9.5 %collective-permute-start.1 = (bf16[2,256,384]{2,1,0:T(8,128)(2,1)S(1)}, bf16[2,256,384]{2,1,0:T(8,128)(2,1)S(1)}, u32[]{:S(2)}, u32[]{:S(2)}) collective-permute-start(bf16[2,256,384]{2,1,0:T(8,128)(2,1)S(1)} %constant_dynamic-update-slice_fusion), channel_id=1, source_target_pairs={{0,8},{8,16},{16,24},{24,32},{32,40},{40,48},{48,56},{56,64},{64,7... | collective-permute-start | bytes 1179656 | tf_op jit(solution)/shard_map/ppermute | solution.py:17
  8.0 8.2 %collective-permute-start.2 = (bf16[2,256,384]{2,1,0:T(8,128)(2,1)S(1)}, bf16[2,256,384]{2,1,0:T(8,128)(2,1)S(1)}, u32[]{:S(2)}, u32[]{:S(2)}) collective-permute-start(bf16[2,256,384]{2,1,0:T(8,128)(2,1)S(1)} %constant_dynamic-update-slice_fusion), channel_id=1, source_target_pairs={{8,0},{16,8},{24,16},{32,24},{40,32},{48,40},{56,48},{64,56},{72,6... | collective-permute-start | bytes 1179656 | tf_op jit(solution)/shard_map/ppermute | solution.py:17
  9.3 18.8 %collective-permute-start.3 = (bf16[2,256,384]{2,1,0:T(8,128)(2,1)S(1)}, bf16[2,256,384]{2,1,0:T(8,128)(2,1)S(1)}, u32[]{:S(2)}, u32[]{:S(2)}) collective-permute-start(bf16[2,256,384]{2,1,0:T(8,128)(2,1)S(1)} %constant_dynamic-update-slice_fusion), channel_id=1, source_target_pairs={{16,0},{24,8},{32,16},{40,24},{48,32},{56,40},{64,48},{72,56},{80,... | collective-permute-start | bytes 1179656 | tf_op jit(solution)/shard_map/ppermute | solution.py:17
  28.2 0.9 copy-start.9
  28.4 2.3 %copy-start.1 = (bf16[1280,384]{1,0:T(8,128)(2,1)}, bf16[1280,384]{1,0:T(8,128)(2,1)S(1)}, u32[]{:S(2)}) copy-start(bf16[1280,384]{1,0:T(8,128)(2,1)S(1)} %get-tuple-element.16) | copy-start | bytes 2949124
  28.4 4.3 %copy-start.5 = (bf16[1280,384]{1,0:T(8,128)(2,1)}, bf16[1280,384]{1,0:T(8,128)(2,1)S(1)}, u32[]{:S(2)}) copy-start(bf16[1280,384]{1,0:T(8,128)(2,1)S(1)} %get-tuple-element.17) | copy-start | bytes 2949124
  32.5 21.3 %copy-start.15 = (f32[384]{0:T(512)S(1)}, f32[384]{0:T(512)}, u32[]{:S(2)}) copy-start(f32[384]{0:T(512)} %param.11) | copy-start | bytes 4612
  77.3 1.6 copy-start.6
  80.5 1.3 copy-start.2
  88.5 2.5 %copy-start.10 = (f32[128,1280]{0,1:T(8,128)S(1)}, f32[128,1280]{0,1:T(8,128)}, u32[]{:S(2)}) copy-start(f32[128,1280]{0,1:T(8,128)} %get-tuple-element.35) | copy-start | bytes 1966084
  90.6 1.0 copy-start.4
  91.6 1.0 copy-start.11
  91.6 1.2 copy-start.12
  91.6 1.3 copy-start.13
  91.6 1.5 copy-start.14
  93.2 1.3 copy-start
  94.5 9.5 %copy-start.3 = (bf16[1280,384]{1,0:T(8,128)(2,1)S(1)}, bf16[1280,384]{1,0:T(8,128)(2,1)}, u32[]{:S(2)}) copy-start(bf16[1280,384]{1,0:T(8,128)(2,1)} %copy-done.1) | copy-start | bytes 2949124
  95.6 67.3 %collective-permute-start.7 = (bf16[2,256,384]{1,2,0:T(8,128)(2,1)}, bf16[2,256,384]{1,2,0:T(8,128)(2,1)S(1)}, u32[]{:S(2)}, u32[]{:S(2)}) collective-permute-start(bf16[2,256,384]{1,2,0:T(8,128)(2,1)} %get-tuple-element.13), channel_id=1, source_target_pairs={{0,16},{8,24},{16,32},{24,40},{32,48},{40,56},{48,64},{56,72},{64,... | collective-permute-start | bytes 1179656 | tf_op jit(solution)/shard_map/ppermute | solution.py:17
  99.4 63.5 %collective-permute-start.6 = (bf16[2,256,384]{1,2,0:T(8,128)(2,1)}, bf16[2,256,384]{1,2,0:T(8,128)(2,1)}, u32[]{:S(2)}, u32[]{:S(2)}) collective-permute-start(bf16[2,256,384]{1,2,0:T(8,128)(2,1)} %get-tuple-element.14), channel_id=1, source_target_pairs={{0,8},{8,16},{16,24},{24,32},{32,40},{40,48},{48,56},{56,64},{64,7... | collective-permute-start | bytes 1179656 | tf_op jit(solution)/shard_map/ppermute | solution.py:17
  101.5 61.4 %collective-permute-start.5 = (bf16[2,256,384]{1,2,0:T(8,128)(2,1)}, bf16[2,256,384]{1,2,0:T(8,128)(2,1)}, u32[]{:S(2)}, u32[]{:S(2)}) collective-permute-start(bf16[2,256,384]{1,2,0:T(8,128)(2,1)} %get-tuple-element.15), channel_id=1, source_target_pairs={{8,0},{16,8},{24,16},{32,24},{40,32},{48,40},{56,48},{64,56},{72,6... | collective-permute-start | bytes 1179656 | tf_op jit(solution)/shard_map/ppermute | solution.py:17
  102.8 60.1 %collective-permute-start.4 = (bf16[2,256,384]{1,2,0:T(8,128)(2,1)S(1)}, bf16[2,256,384]{1,2,0:T(8,128)(2,1)}, u32[]{:S(2)}, u32[]{:S(2)}) collective-permute-start(bf16[2,256,384]{1,2,0:T(8,128)(2,1)S(1)} %get-tuple-element.12), channel_id=1, source_target_pairs={{16,0},{24,8},{32,16},{40,24},{48,32},{56,40},{64,48},{72,56},{80,... | collective-permute-start | bytes 1179656 | tf_op jit(solution)/shard_map/ppermute | solution.py:17
